TPU v7x, 32 devices: a whole 2x2x4 slice. The times are simulated.
32 devices in a mesh: fsdp: 8 (over z, x), replica: 4 (over y, core).
Axes of the slice: x: 2, y: 2, z: 4, core: 2. Of those that a mesh axis runs over, the one named last changes fastest.
Arguments:
- layer_input: bfloat16 [32, 1024, 768], P(('fsdp', 'replica')), may hold values from -6 to 6
- cotangent: bfloat16 [32, 1024, 768], P(('fsdp', 'replica')), may hold values from -6 to 6
- segment_ids: int32 [32, 1024], P(('fsdp', 'replica')), may hold values from 0 to 4, as said below
- pad_mask: int32 [32, 1024], P(('fsdp', 'replica')), may hold values from 0 to 1, as said below
- ln1_gain: bfloat16 [768], P('fsdp'), may hold values from 0.5 to 1.5
- ln1_bias: bfloat16 [768], P('fsdp'), may hold values from -1.1953125 to 1.1953125
- w_qkv: bfloat16 [768, 2304], P('fsdp'), may hold values from -0.21875 to 0.21875
- b_qkv: bfloat16 [2304], P('fsdp'), may hold values from -1.1953125 to 1.1953125
- w_out: bfloat16 [768, 768], P('fsdp'), may hold values from -1.25 to 1.25
- b_out: bfloat16 [768], P('fsdp'), may hold values from -1.1953125 to 1.1953125
- ln2_gain: bfloat16 [768], P('fsdp'), may hold values from 0.5 to 1.5
- ln2_bias: bfloat16 [768], P('fsdp'), may hold values from -1.1953125 to 1.1953125
- w_up: bfloat16 [768, 3072], P('fsdp'), may hold values from -0.21875 to 0.21875
- b_up: bfloat16 [3072], P('fsdp'), may hold values from -1.1953125 to 1.1953125
- w_down: bfloat16 [3072, 768], P('fsdp'), may hold values from -0.109375 to 0.109375
- b_down: bfloat16 [768], P('fsdp'), may hold values from -1.1953125 to 1.1953125
Outputs:
- layer_out: bfloat16 [32, 1024, 768], P(('fsdp', 'replica'))
- input_grad: bfloat16 [32, 1024, 768], P(('fsdp', 'replica'))
- grad_ln1_gain: float32 [768], P('fsdp')
- grad_ln1_bias: float32 [768], P('fsdp')
- grad_w_qkv: float32 [768, 2304], P('fsdp')
- grad_b_qkv: float32 [2304], P('fsdp')
- grad_w_out: float32 [768, 768], P('fsdp')
- grad_b_out: float32 [768], P('fsdp')
- grad_ln2_gain: float32 [768], P('fsdp')
- grad_ln2_bias: float32 [768], P('fsdp')
- grad_w_up: float32 [768, 3072], P('fsdp')
- grad_b_up: float32 [3072], P('fsdp')
- grad_w_down: float32 [3072, 768], P('fsdp')
- grad_b_down: float32 [768], P('fsdp')
Inputs may be any that keep to these rules, and one draw needn't show every extreme that they name: `segment_ids`: each row packs 4 genes numbered 0 to 3 in order from its start, each of 128 to 256 codons, never falling along a row, and 4 on the padded tail; in every row one gene has exactly 256 codons and another exactly 128. `pad_mask`: 1 exactly where segment_ids is under 4; every row ends in at least 128 padded codons.
All inputs are finite; a program needn't handle non-finite values.
Results may differ from a plain program's by a relative error of at most 0.014.
Values may be sent and summed in bfloat16 or wider, within the bound.
No kernel may reach another device: no remote copies, remote signals or barrier semaphores. Data moves between devices by JAX's collectives and lax.ppermute only.
A program may use at most 320 MiB of HBM per device.

v0:
```python
import math
import jax
import jax.numpy as jnp
from jax import lax
from jax.sharding import PartitionSpec as P

HEADS = 12
HEAD_DIM = 64
GENES = 4
EPSILON = 1e-05
NEG_FILL = -1000000000.0


def contract_rows(left_matrix, right_matrix):
    return lax.dot_general(
        left_matrix, right_matrix, (((0,), (0,)), ((), ())), preferred_element_type=jnp.float32
    )


def times_transpose(left_matrix, right_matrix):
    return lax.dot_general(
        left_matrix, right_matrix, (((1,), (1,)), ((), ())), preferred_element_type=jnp.float32
    )


def layer_norm(inputs, gain_vector, bias_vector):
    centered = inputs - jnp.mean(inputs, -1, keepdims=True)
    variance = jnp.mean(centered * centered, -1, keepdims=True)
    return centered * lax.rsqrt(variance + EPSILON) * gain_vector + bias_vector


def rotate(tensor, cosine_table, sine_table):
    half_dim = tensor.shape[-1] // 2
    first_half = tensor[..., :half_dim]
    second_half = tensor[..., half_dim:]
    return jnp.concatenate(
        [
            first_half * cosine_table - second_half * sine_table,
            second_half * cosine_table + first_half * sine_table,
        ],
        -1,
    )


def exact_gelu(inputs):
    return jax.nn.gelu(inputs, approximate=False)


def rotary_tables(positions):
    frequency = jnp.power(10000.0, jnp.arange(HEAD_DIM // 2, dtype=jnp.float32) * (-2.0 / HEAD_DIM))
    angles = positions.astype(jnp.float32)[..., None] * frequency
    return (jnp.cos(angles)[..., None, :], jnp.sin(angles)[..., None, :])


def gene_positions(segments):
    slot_ids = jnp.arange(GENES + 1, dtype=jnp.int32)
    slot_hits = segments[..., :, None] == slot_ids
    counts = jnp.sum(slot_hits.astype(jnp.int32), -2)
    starts = jnp.cumsum(counts, -1) - counts
    gene_start = jnp.sum(jnp.where(slot_hits, starts[..., None, :], 0), -1)
    return jnp.arange(segments.shape[-1], dtype=jnp.int32) - gene_start


def pair_mask(block_segments, block_valid, block_start, segments, valid_codons):
    row_ids = block_start + jnp.arange(block_segments.shape[0], dtype=jnp.int32)
    column_ids = jnp.arange(segments.shape[0], dtype=jnp.int32)
    same_gene = (
        (block_segments[:, None] == segments[None, :])
        & (block_valid[:, None] > 0)
        & (valid_codons[None, :] > 0)
    )
    return same_gene | (row_ids[:, None] == column_ids[None, :])


def block_scores(
    block_queries, key_rows, block_segments, block_valid, block_start, segments, valid_codons
):
    scores = jnp.einsum(
        "qhd,khd->hqk", block_queries, key_rows, preferred_element_type=jnp.float32
    ) * (1.0 / math.sqrt(HEAD_DIM))
    allowed = pair_mask(block_segments, block_valid, block_start, segments, valid_codons)
    return jnp.where(allowed[None], scores, NEG_FILL)


def split_blocks(queries, segments, valid_codons, block_rows):
    block_count = queries.shape[0] // block_rows
    starts = jnp.arange(block_count, dtype=jnp.int32) * block_rows
    return (
        queries.reshape(block_count, block_rows, HEADS, HEAD_DIM),
        segments.reshape(block_count, block_rows),
        valid_codons.reshape(block_count, block_rows),
        starts,
    )


def attend_forward(queries, key_rows, value_rows, segments, valid_codons, block_rows):
    length = queries.shape[0]

    def one_block(running, block_item):
        block_queries, block_segments, block_valid, block_start = block_item
        scores = block_scores(
            block_queries,
            key_rows,
            block_segments,
            block_valid,
            block_start,
            segments,
            valid_codons,
        )
        row_peak = jnp.max(scores, -1, keepdims=True)
        shifted = jnp.exp(scores - row_peak)
        row_total = jnp.sum(shifted, -1, keepdims=True)
        weights = (shifted / row_total).astype(jnp.bfloat16)
        attended = jnp.einsum(
            "hqk,khd->qhd", weights, value_rows, preferred_element_type=jnp.float32
        )
        log_total = (row_peak + jnp.log(row_total))[..., 0]
        return (running, (attended, log_total))

    ignored, (attended, log_total) = lax.scan(
        one_block,
        jnp.zeros((), jnp.float32),
        split_blocks(queries, segments, valid_codons, block_rows),
    )
    return (attended.reshape(length, HEADS, HEAD_DIM), log_total)


def attend_backward(
    queries, key_rows, value_rows, attended_grad, log_total, segments, valid_codons, block_rows
):
    length = queries.shape[0]
    block_queries_all, block_segments_all, block_valid_all, starts = split_blocks(
        queries, segments, valid_codons, block_rows
    )
    grad_blocks = attended_grad.reshape(block_queries_all.shape)
    score_scale = 1.0 / math.sqrt(HEAD_DIM)

    def one_block(running, block_item):
        key_grad, value_grad = running
        block_queries, block_grad, block_log, block_segments, block_valid, block_start = block_item
        scores = block_scores(
            block_queries,
            key_rows,
            block_segments,
            block_valid,
            block_start,
            segments,
            valid_codons,
        )
        weights = jnp.exp(scores - block_log[..., None])
        weight_grad = jnp.einsum(
            "qhd,khd->hqk", block_grad, value_rows, preferred_element_type=jnp.float32
        )
        row_dot = jnp.sum(weights * weight_grad, -1, keepdims=True)
        score_grad = (weights * (weight_grad - row_dot)).astype(jnp.bfloat16)
        query_grad = (
            jnp.einsum("hqk,khd->qhd", score_grad, key_rows, preferred_element_type=jnp.float32)
            * score_scale
        )
        key_grad = (
            key_grad
            + jnp.einsum(
                "hqk,qhd->khd", score_grad, block_queries, preferred_element_type=jnp.float32
            )
            * score_scale
        )
        value_grad = value_grad + jnp.einsum(
            "hqk,qhd->khd",
            weights.astype(jnp.bfloat16),
            block_grad,
            preferred_element_type=jnp.float32,
        )
        return ((key_grad, value_grad), query_grad)

    zero_grad = jnp.zeros(key_rows.shape, jnp.float32)
    scanned = (
        block_queries_all,
        grad_blocks,
        log_total,
        block_segments_all,
        block_valid_all,
        starts,
    )
    (key_grad, value_grad), query_grad = lax.scan(one_block, (zero_grad, zero_grad), scanned)
    return (query_grad.reshape(length, HEADS, HEAD_DIM), key_grad, value_grad)


def body(
    layer_input,
    cotangent,
    segment_ids,
    pad_mask,
    ln1_gain,
    ln1_bias,
    w_qkv,
    b_qkv,
    w_out,
    b_out,
    ln2_gain,
    ln2_bias,
    w_up,
    b_up,
    w_down,
    b_down,
):
    gain_one, bias_one, qkv_weight, qkv_bias, out_weight, out_bias = (
        lax.all_gather(ln1_gain, "fsdp", axis=0, tiled=True),
        lax.all_gather(ln1_bias, "fsdp", axis=0, tiled=True),
        lax.all_gather(w_qkv, "fsdp", axis=0, tiled=True),
        lax.all_gather(b_qkv, "fsdp", axis=0, tiled=True),
        lax.all_gather(w_out, "fsdp", axis=0, tiled=True),
        lax.all_gather(b_out, "fsdp", axis=0, tiled=True),
    )
    gain_two, bias_two, up_weight, up_bias, down_weight, down_bias = (
        lax.all_gather(ln2_gain, "fsdp", axis=0, tiled=True),
        lax.all_gather(ln2_bias, "fsdp", axis=0, tiled=True),
        lax.all_gather(w_up, "fsdp", axis=0, tiled=True),
        lax.all_gather(b_up, "fsdp", axis=0, tiled=True),
        lax.all_gather(w_down, "fsdp", axis=0, tiled=True),
        lax.all_gather(b_down, "fsdp", axis=0, tiled=True),
    )
    length = layer_input.shape[1]
    model_width = layer_input.shape[2]
    block_rows = min(512, length)
    segments = segment_ids[0]
    valid_codons = pad_mask[0]
    cosine_table, sine_table = rotary_tables(gene_positions(segments))
    inputs = layer_input[0].astype(jnp.float32)
    normed, norm_one_back = jax.vjp(
        layer_norm, inputs, gain_one.astype(jnp.float32), bias_one.astype(jnp.float32)
    )
    normed = normed.astype(jnp.bfloat16)
    projected = jnp.dot(normed, qkv_weight, preferred_element_type=jnp.float32) + qkv_bias.astype(
        jnp.float32
    )
    head_shape = (length, HEADS, HEAD_DIM)
    queries = rotate(
        projected[:, :model_width].reshape(head_shape), cosine_table, sine_table
    ).astype(jnp.bfloat16)
    key_rows = rotate(
        projected[:, model_width : 2 * model_width].reshape(head_shape), cosine_table, sine_table
    ).astype(jnp.bfloat16)
    value_rows = projected[:, 2 * model_width :].reshape(head_shape).astype(jnp.bfloat16)
    attended, log_total = attend_forward(
        queries, key_rows, value_rows, segments, valid_codons, block_rows
    )
    attended = attended.reshape(length, model_width).astype(jnp.bfloat16)
    middle = (
        inputs
        + jnp.dot(attended, out_weight, preferred_element_type=jnp.float32)
        + out_bias.astype(jnp.float32)
    )
    normed_two, norm_two_back = jax.vjp(
        layer_norm, middle, gain_two.astype(jnp.float32), bias_two.astype(jnp.float32)
    )
    normed_two = normed_two.astype(jnp.bfloat16)
    hidden = jnp.dot(normed_two, up_weight, preferred_element_type=jnp.float32) + up_bias.astype(
        jnp.float32
    )
    activated, gelu_back = jax.vjp(exact_gelu, hidden)
    activated = activated.astype(jnp.bfloat16)
    layer_out = (
        middle
        + jnp.dot(activated, down_weight, preferred_element_type=jnp.float32)
        + down_bias.astype(jnp.float32)
    ).astype(jnp.bfloat16)
    up_weight_back, down_weight_back = (
        lax.all_gather(w_up, "fsdp", axis=0, tiled=True),
        lax.all_gather(w_down, "fsdp", axis=0, tiled=True),
    )
    out_grad_rows = cotangent[0]
    grad_down_bias = jnp.sum(out_grad_rows.astype(jnp.float32), 0)
    (hidden_grad,) = gelu_back(times_transpose(out_grad_rows, down_weight_back))
    hidden_grad = hidden_grad.astype(jnp.bfloat16)
    grad_up_bias = jnp.sum(hidden_grad.astype(jnp.float32), 0)
    middle_grad, grad_gain_two, grad_bias_two = norm_two_back(
        times_transpose(hidden_grad, up_weight_back)
    )
    middle_grad = middle_grad + out_grad_rows.astype(jnp.float32)
    grad_up_weight = contract_rows(normed_two, hidden_grad)
    grad_down_weight = contract_rows(activated, out_grad_rows)
    ffn_sums = (
        lax.psum_scatter(grad_gain_two, "fsdp", scatter_dimension=0, tiled=True),
        lax.psum_scatter(grad_bias_two, "fsdp", scatter_dimension=0, tiled=True),
        lax.psum_scatter(grad_up_weight, "fsdp", scatter_dimension=0, tiled=True),
        lax.psum_scatter(grad_up_bias, "fsdp", scatter_dimension=0, tiled=True),
        lax.psum_scatter(grad_down_weight, "fsdp", scatter_dimension=0, tiled=True),
        lax.psum_scatter(grad_down_bias, "fsdp", scatter_dimension=0, tiled=True),
    )
    qkv_weight_back, out_weight_back = (
        lax.all_gather(w_qkv, "fsdp", axis=0, tiled=True),
        lax.all_gather(w_out, "fsdp", axis=0, tiled=True),
    )
    branch_grad = middle_grad.astype(jnp.bfloat16)
    grad_out_bias = jnp.sum(branch_grad.astype(jnp.float32), 0)
    attended_grad = (
        times_transpose(branch_grad, out_weight_back).astype(jnp.bfloat16).reshape(head_shape)
    )
    query_grad, key_grad, value_grad = attend_backward(
        queries, key_rows, value_rows, attended_grad, log_total, segments, valid_codons, block_rows
    )
    projected_grad = jnp.concatenate(
        [
            rotate(query_grad, cosine_table, -sine_table).reshape(length, model_width),
            rotate(key_grad, cosine_table, -sine_table).reshape(length, model_width),
            value_grad.reshape(length, model_width),
        ],
        1,
    ).astype(jnp.bfloat16)
    grad_qkv_bias = jnp.sum(projected_grad.astype(jnp.float32), 0)
    input_part, grad_gain_one, grad_bias_one = norm_one_back(
        times_transpose(projected_grad, qkv_weight_back)
    )
    input_grad = (middle_grad + input_part).astype(jnp.bfloat16)
    grad_out_weight = contract_rows(attended, branch_grad)
    grad_qkv_weight = contract_rows(normed, projected_grad)
    attn_sums = (
        lax.psum_scatter(grad_gain_one, "fsdp", scatter_dimension=0, tiled=True),
        lax.psum_scatter(grad_bias_one, "fsdp", scatter_dimension=0, tiled=True),
        lax.psum_scatter(grad_qkv_weight, "fsdp", scatter_dimension=0, tiled=True),
        lax.psum_scatter(grad_qkv_bias, "fsdp", scatter_dimension=0, tiled=True),
        lax.psum_scatter(grad_out_weight, "fsdp", scatter_dimension=0, tiled=True),
        lax.psum_scatter(grad_out_bias, "fsdp", scatter_dimension=0, tiled=True),
    )
    reduced = (
        lax.psum(attn_sums[0].astype(jnp.bfloat16), "replica").astype(jnp.float32),
        lax.psum(attn_sums[1].astype(jnp.bfloat16), "replica").astype(jnp.float32),
        lax.psum(attn_sums[2].astype(jnp.bfloat16), "replica").astype(jnp.float32),
        lax.psum(attn_sums[3].astype(jnp.bfloat16), "replica").astype(jnp.float32),
        lax.psum(attn_sums[4].astype(jnp.bfloat16), "replica").astype(jnp.float32),
        lax.psum(attn_sums[5].astype(jnp.bfloat16), "replica").astype(jnp.float32),
        lax.psum(ffn_sums[0].astype(jnp.bfloat16), "replica").astype(jnp.float32),
        lax.psum(ffn_sums[1].astype(jnp.bfloat16), "replica").astype(jnp.float32),
        lax.psum(ffn_sums[2].astype(jnp.bfloat16), "replica").astype(jnp.float32),
        lax.psum(ffn_sums[3].astype(jnp.bfloat16), "replica").astype(jnp.float32),
        lax.psum(ffn_sums[4].astype(jnp.bfloat16), "replica").astype(jnp.float32),
        lax.psum(ffn_sums[5].astype(jnp.bfloat16), "replica").astype(jnp.float32),
    )
    return (
        layer_out[None],
        input_grad[None],
        reduced[0],
        reduced[1],
        reduced[2],
        reduced[3],
        reduced[4],
        reduced[5],
        reduced[6],
        reduced[7],
        reduced[8],
        reduced[9],
        reduced[10],
        reduced[11],
    )


def solution(mesh):
    in_specs = (
        P(("fsdp", "replica"), None, None),
        P(("fsdp", "replica"), None, None),
        P(("fsdp", "replica"), None),
        P(("fsdp", "replica"), None),
        P("fsdp"),
        P("fsdp"),
        P("fsdp", None),
        P("fsdp"),
        P("fsdp", None),
        P("fsdp"),
        P("fsdp"),
        P("fsdp"),
        P("fsdp", None),
        P("fsdp"),
        P("fsdp", None),
        P("fsdp"),
    )
    out_specs = (
        P(("fsdp", "replica"), None, None),
        P(("fsdp", "replica"), None, None),
        P("fsdp"),
        P("fsdp"),
        P("fsdp", None),
        P("fsdp"),
        P("fsdp", None),
        P("fsdp"),
        P("fsdp"),
        P("fsdp"),
        P("fsdp", None),
        P("fsdp"),
        P("fsdp", None),
        P("fsdp"),
    )
    return jax.shard_map(body, mesh=mesh, in_specs=in_specs, out_specs=out_specs, check_vma=False)
```

profile of v0, /device:TPU:0, one launch (start us, length us, event | category | flops | bytes accessed | tf_op | source)
XLA Modules:
  0.0 1118.5 jit_solution(7735304638543786908)
XLA Ops:
  24.4 39.9 %all-reduce.16 = (bf16[768]{0:T(1024)(128)(2,1)}, bf16[2304]{0:T(1024)(128)(2,1)S(1)}, bf16[768]{0:T(1024)(128)(2,1)S(1)}, bf16[768]{0:T(1024)(128)(2,1)S(1)}, b...) all-reduce(bf16[768]{0:T(1024)(128)(2,1)S(1)} %dynamic-update-slice, ...), channel_id=1, replica_groups=mesh['fsdp'=8,'replica'=4] {'fsdp'}, use_global_device_ids=true, to_apply=%add.6 | all-reduce | flops 6912 | bytes 27648
  66.0 25.9 %all-gather = bf16[8,1,384]{2,1,0:T(2,128)(2,1)S(1)} all-gather(bf16[1,1,384]{2,1,0:T(2,128)(2,1)S(1)} %reshape.495), channel_id=1, replica_groups=mesh['fsdp'=8,'replica'=4] {'fsdp'}, dimensions={0}, use_global_device_ids=true | all-gather | bytes 6912 | tf_op jit(solution)/shard_map/all_gather | solution.py:218
  98.7 6.3 convolution_add_fusion
  106.3 3.0 fusion.72
  109.3 2.4 copy.88
  111.7 2.6 copy.89
  114.3 3.6 copy.85
  117.9 2.9 subtract_convert_fusion.2
  121.5 74.1 %while.27 = (s32[]{:T(128)}, bf16[2,512,12,64]{1,3,2,0:T(8,128)(2,1)}, f32[2,12,512]{2,1,0:T(8,128)S(1)}, s32[2,512]{1,0:T(2,128)S(1)}, s32[1,1024]{1,0:T(1,128)...) while((s32[]{:T(128)}, ...), condition=%wide.region_8.9_spmd, body=%wide.region_5.8_spmd.sunk | while | flops 1688727552 | bytes 190299344 | solution.py:120
  123.7 11.0 fusion.120
  134.7 12.4 %fusion.121 = f32[12,512]{1,0:T(8,128)S(1)} fusion(f32[12,512,1024]{2,1,0:T(8,128)} %get-tuple-element.584, f32[12,512]{1,0:T(8,128)S(1)} %get-tuple-element.585, pred[512,1024]{1,0:T(8,128)(4,1)S(1)} %fusion.119), kind=kLoop, calls=%fused_computation.4.clone.1 | loop fusion | flops 25159680 | bytes 25739264 | tf_op jit(solution)/shard_map/while/body/eval_jaxpr/reduce_sum | solution.py:112
  147.1 3.2 copy-done
  150.3 8.5 bitcast_dynamic-update-slice_fusion.6
  160.8 10.7 fusion.120
  171.5 12.3 %fusion.121 = f32[12,512]{1,0:T(8,128)S(1)} fusion(f32[12,512,1024]{2,1,0:T(8,128)} %get-tuple-element.584, f32[12,512]{1,0:T(8,128)S(1)} %get-tuple-element.585, pred[512,1024]{1,0:T(8,128)(4,1)S(1)} %fusion.119), kind=kLoop, calls=%fused_computation.4.clone.1 | loop fusion | flops 25159680 | bytes 25739264 | tf_op jit(solution)/shard_map/while/body/eval_jaxpr/reduce_sum | solution.py:112
  183.8 3.3 copy-done
  187.1 8.5 bitcast_dynamic-update-slice_fusion.6
  195.7 4.1 copy.90
  201.5 3.8 fusion.74
  206.1 37.9 %multiply_convert_fusion.1 = (bf16[1024,3072]{1,0:T(8,128)(2,1)}, f32[1024,3072]{1,0:T(8,128)}, f32[1024,3072]{1,0:T(8,128)}) fusion(f32[3072]{0:T(1024)S(1)} %bitcast.217, bf16[768,3072]{1,0:T(8,128)(2,1)} %all-gather.10.cloned.1.call-done, f32[1024,768]{0,1:T(8,128)S(1)} %get-tuple-element.432, f32[768]{0:T(1024)S(1)} %copy-done.60, ...), kind=kOutput, calls=%fused_computation.56 | convolution fusion | flops 5043388416 | bytes 39348224 | tf_op jit(solution)/shard_map/dot_general | solution.py:257
  244.0 37.8 %all-gather.12.cloned.1.call-done = bf16[3072,768]{1,0:T(8,128)(2,1)} async-done(((bf16[384,768]{1,0:T(8,128)(2,1)}), bf16[3072,768]{1,0:T(8,128)(2,1)}) %all-gather.12.cloned.1.call-update) | async-done | bytes 4718608 | tf_op jit(solution)/shard_map/all_gather | solution.py:219
  281.8 19.1 %convert_reduce_fusion = (f32[3072]{0:T(1024)}, bf16[1024,3072]{1,0:T(8,128)(2,1)}) fusion(f32[1024,3072]{1,0:T(8,128)} %get-tuple-element.405, bf16[3072,768]{1,0:T(8,128)(2,1)} %all-gather.12.cloned.1.call-done, bf16[1,1024,768]{2,1,0:T(8,128)(2,1)} %param.21, f32[1024,3072]{1,0:T(8,128)} %get-tuple-element.433, f32[3072]{0:T(1024)S(1)} %bitcast.218), kind=kOutput, calls=%fused_computation.54 | convolution fusion | flops 4885312512 | bytes 37773312 | tf_op jit(solution)/shard_map/dot_general | solution.py:21
  300.9 10.4 fusion.76
  311.3 3.5 copy.93
  314.8 3.5 multiply_reduce_fusion.1
  321.8 2.8 fusion.77
  324.6 2.7 convolution_convert_fusion
  331.0 233.6 %while.28 = (s32[]{:T(128)}, f32[1024,12,64]{0,2,1:T(8,128)}, f32[1024,12,64]{0,2,1:T(8,128)}, f32[2,512,12,64]{1,0,3,2:T(2,128)}, bf16[2,512,12,64]{1,3,2,0:T(8...) while((s32[]{:T(128)}, f32[1024,12,64]{0,2,1:T(8,128)}, ...), condition=%wide.region_15.16_spmd.clone, body=%wide.region_13.15_spmd.clone.sunk | while | flops 4127846400 | bytes 238230832 | solution.py:184
  333.2 11.4 %fusion.131 = f32[12,512,1024]{2,1,0:T(8,128)} fusion(bf16[1024,12,64]{0,2,1:T(8,128)(2,1)S(1)} %get-tuple-element.680, bf16[2,512,12,64]{1,3,2,0:T(8,128)(2,1)} %get-tuple-element.674, s32[]{:T(128)S(6)} %copy.152), kind=kOutput, calls=%fused_computation.35.clone.1 | convolution fusion | flops 805306368 | bytes 27525124 | tf_op jit(solution)/shard_map/while/body/eval_jaxpr/qhd,khd->hqk/dot_general | solution.py:78
  344.7 13.8 %bitcast_add_fusion.5 = f32[1024,12,64]{0,2,1:T(8,128)} fusion(f32[1024,12,64]{0,2,1:T(8,128)} %get-tuple-element.656, f32[12,512,1024]{2,1,0:T(8,128)} %fusion.131, f32[12,512]{1,0:T(8,128)S(1)} %dynamic-slice_bitcast_fusion.2, pred[512,1024]{1,0:T(8,128)(4,1)S(1)} %fusion.132, pred[]{:T(512)S(6)} %compare.3, ...), kind=kOutput, calls=%fused_computation.26.clone.1 | convolution fusion | flops 832045056 | bytes 32800772 | tf_op jit(solution)/shard_map/while/body/eval_jaxpr/hqk,qhd->khd/dot_general | solution.py:167
  358.5 18.2 %multiply_reduce_fusion.5 = (f32[12,512]{1,0:T(8,128)S(1)}, f32[12,512,1024]{2,1,0:T(8,128)}) fusion(f32[12,512,1024]{2,1,0:T(8,128)} %fusion.131, f32[12,512]{1,0:T(8,128)S(1)} %dynamic-slice_bitcast_fusion.2, pred[512,1024]{1,0:T(8,128)(4,1)S(1)} %fusion.132, bf16[1024,12,64]{0,2,1:T(8,128)(2,1)} %get-tuple-element.683, ...), kind=kOutput, calls=%fused_computation.21.clone.1 | convolution fusion | flops 836757504 | bytes 53264388 | tf_op jit(solution)/shard_map/while/body/eval_jaxpr/qhd,khd->hqk/dot_general | solution.py:151
  376.7 21.7 %multiply_convert_fusion.3 = bf16[12,512,1024]{2,1,0:T(8,128)(2,1)} fusion(f32[12,512,1024]{2,1,0:T(8,128)} %get-tuple-element.600, f32[12,512,1024]{2,1,0:T(8,128)} %fusion.131, f32[12,512]{1,0:T(8,128)S(1)} %get-tuple-element.601, f32[12,512]{1,0:T(8,128)S(1)} %dynamic-slice_bitcast_fusion.2, pred[512,1024]{1,0:T(8,128)(4,1)S(1)} %fusion.132), kind=kLoop, calls=%fused_computation.20.clone.1 | loop fusion | flops 37748736 | bytes 63488000 | tf_op jit(solution)/shard_map/while/body/eval_jaxpr/convert_element_type | solution.py:155
  398.4 9.8 multiply_bitcast_fusion.2
  408.2 8.7 bitcast_add_fusion.4
  418.6 28.8 %dynamic_update_slice.19 = f32[2,512,12,64]{1,0,3,2:T(2,128)} dynamic-update-slice(f32[2,512,12,64]{1,0,3,2:T(2,128)} %get-tuple-element.657, f32[1,512,12,64]{1,0,3,2:T(1,128)S(1)} %copy.127, s32[]{:T(128)S(6)} %copy.152, s32[]{:T(128)} %constant.33.clone.1..sunk, s32[]{:T(128)} %constant.33.clone.1..sunk, s32[]{:T(128)} %constant.33.clone.1..sunk) | dynamic-update-slice | bytes 3145732 | tf_op jit(solution)/shard_map/while/body/jit(dynamic_update_index_in_dim)/dynamic_update_slice | solution.py:120
  449.4 11.4 %fusion.131 = f32[12,512,1024]{2,1,0:T(8,128)} fusion(bf16[1024,12,64]{0,2,1:T(8,128)(2,1)S(1)} %get-tuple-element.680, bf16[2,512,12,64]{1,3,2,0:T(8,128)(2,1)} %get-tuple-element.674, s32[]{:T(128)S(6)} %copy.152), kind=kOutput, calls=%fused_computation.35.clone.1 | convolution fusion | flops 805306368 | bytes 27525124 | tf_op jit(solution)/shard_map/while/body/eval_jaxpr/qhd,khd->hqk/dot_general | solution.py:78
  460.8 14.3 %bitcast_add_fusion.5 = f32[1024,12,64]{0,2,1:T(8,128)} fusion(f32[1024,12,64]{0,2,1:T(8,128)} %get-tuple-element.656, f32[12,512,1024]{2,1,0:T(8,128)} %fusion.131, f32[12,512]{1,0:T(8,128)S(1)} %dynamic-slice_bitcast_fusion.2, pred[512,1024]{1,0:T(8,128)(4,1)S(1)} %fusion.132, pred[]{:T(512)S(6)} %compare.3, ...), kind=kOutput, calls=%fused_computation.26.clone.1 | convolution fusion | flops 832045056 | bytes 32800772 | tf_op jit(solution)/shard_map/while/body/eval_jaxpr/hqk,qhd->khd/dot_general | solution.py:167
  475.1 18.1 %multiply_reduce_fusion.5 = (f32[12,512]{1,0:T(8,128)S(1)}, f32[12,512,1024]{2,1,0:T(8,128)}) fusion(f32[12,512,1024]{2,1,0:T(8,128)} %fusion.131, f32[12,512]{1,0:T(8,128)S(1)} %dynamic-slice_bitcast_fusion.2, pred[512,1024]{1,0:T(8,128)(4,1)S(1)} %fusion.132, bf16[1024,12,64]{0,2,1:T(8,128)(2,1)} %get-tuple-element.683, ...), kind=kOutput, calls=%fused_computation.21.clone.1 | convolution fusion | flops 836757504 | bytes 53264388 | tf_op jit(solution)/shard_map/while/body/eval_jaxpr/qhd,khd->hqk/dot_general | solution.py:151
  493.2 21.2 %multiply_convert_fusion.3 = bf16[12,512,1024]{2,1,0:T(8,128)(2,1)} fusion(f32[12,512,1024]{2,1,0:T(8,128)} %get-tuple-element.600, f32[12,512,1024]{2,1,0:T(8,128)} %fusion.131, f32[12,512]{1,0:T(8,128)S(1)} %get-tuple-element.601, f32[12,512]{1,0:T(8,128)S(1)} %dynamic-slice_bitcast_fusion.2, pred[512,1024]{1,0:T(8,128)(4,1)S(1)} %fusion.132), kind=kLoop, calls=%fused_computation.20.clone.1 | loop fusion | flops 37748736 | bytes 63488000 | tf_op jit(solution)/shard_map/while/body/eval_jaxpr/convert_element_type | solution.py:155
  514.4 9.8 multiply_bitcast_fusion.2
  524.2 9.6 bitcast_add_fusion.4
  535.4 28.8 %dynamic_update_slice.19 = f32[2,512,12,64]{1,0,3,2:T(2,128)} dynamic-update-slice(f32[2,512,12,64]{1,0,3,2:T(2,128)} %get-tuple-element.657, f32[1,512,12,64]{1,0,3,2:T(1,128)S(1)} %copy.127, s32[]{:T(128)S(6)} %copy.152, s32[]{:T(128)} %constant.33.clone.1..sunk, s32[]{:T(128)} %constant.33.clone.1..sunk, s32[]{:T(128)} %constant.33.clone.1..sunk) | dynamic-update-slice | bytes 3145732 | tf_op jit(solution)/shard_map/while/body/jit(dynamic_update_index_in_dim)/dynamic_update_slice | solution.py:120
  564.6 4.3 reshape.470
  568.9 2.3 convert.46
  574.8 7.0 fusion.63
  582.5 10.5 fusion.67
  594.4 10.2 fusion.55
  607.0 8.6 fusion.75
  615.6 3.7 copy.97
  619.3 2.7 fusion.51
  624.0 9.5 fusion.58
  635.1 74.5 %reduce-scatter.5.cloned.1.call-done = f32[96,2304]{1,0:T(8,128)} async-done(((f32[768,2304]{1,0:T(8,128)}), f32[96,2304]{1,0:T(8,128)}) %reduce-scatter.5.cloned.1.call-update) | async-done | bytes 884752 | tf_op jit(solution)/shard_map/reduce_scatter | solution.py:320
  711.6 164.6 %reduce-scatter.9.cloned.1.call-done = f32[96,3072]{1,0:T(8,128)} async-done(((f32[768,3072]{1,0:T(8,128)}), f32[96,3072]{1,0:T(8,128)}) %reduce-scatter.9.cloned.1.call-update) | async-done | bytes 1179664 | tf_op jit(solution)/shard_map/reduce_scatter | solution.py:285
  876.2 2.2 convert_element_type.214
  878.3 164.5 %reduce-scatter.11.cloned.1.call-done = f32[384,768]{1,0:T(8,128)} async-done(((f32[3072,768]{1,0:T(8,128)}), f32[384,768]{1,0:T(8,128)}) %reduce-scatter.11.cloned.1.call-update) | async-done | bytes 1179664 | tf_op jit(solution)/shard_map/reduce_scatter | solution.py:287
  1042.8 2.1 convert_element_type.219
  1045.0 2.8 convert_reduce_fusion.1
  1047.8 2.6 copy.100
  1050.5 5.9 convert_reduce_fusion.2
  1056.4 35.3 %all-reduce.15 = (bf16[768]{0:T(1024)(128)(2,1)S(1)}, bf16[768]{0:T(1024)(128)(2,1)S(1)}, bf16[2304]{0:T(1024)(128)(2,1)S(1)}, bf16[768]{0:T(1024)(128)(2,1)S(1)...) all-reduce(f32[768]{0:T(1024)S(1)} %get-tuple-element.321, ...), channel_id=2, replica_groups=mesh['fsdp'=8,'replica'=4] {'fsdp'}, use_global_device_ids=true, to_apply=%region_19.20.clone | all-reduce | flops 9984 | bytes 59904
  1092.3 5.7 all-reduce.17
  1102.3 2.6 copy.101
  1106.6 2.0 convert_element_type.201
  1108.6 2.2 convert_element_type.215
  (285 shorter events, 65.7 us)
Async XLA Ops:
  7.2 91.5 %all-gather.6.cloned.1.call-start = ((), (), s32[]{:S(2)}) async-start(), calls=%async_computation.4 | async-start | bytes 3981312 | tf_op jit(solution)/shard_map/all_gather | solution.py:209
  7.9 193.5 %all-gather.8.cloned.1.call-start = ((), (), s32[]{:S(2)}) async-start(), calls=%async_computation.5 | async-start | bytes 1327104 | tf_op jit(solution)/shard_map/all_gather | solution.py:211
  8.7 197.1 %all-gather.10.cloned.1.call-start = ((), (), s32[]{:S(2)}) async-start(), calls=%async_computation.6 | async-start | bytes 5308416 | tf_op jit(solution)/shard_map/all_gather | solution.py:217
  9.4 272.4 %all-gather.12.cloned.1.call-start = ((), (), s32[]{:S(2)}) async-start(), calls=%async_computation.7 | async-start | bytes 5308416 | tf_op jit(solution)/shard_map/all_gather | solution.py:219
  10.0 623.5 %reduce-scatter.7.cloned.1.call-start = ((), (), s32[]{:S(2)}) async-start(), calls=%async_computation.9 | async-start | bytes 2654208 | tf_op jit(solution)/shard_map/reduce_scatter | solution.py:322
  64.2 34.4 %copy-start.41 = (f32[768]{0:T(1024)}, f32[768]{0:T(1024)S(1)}, u32[]{:S(2)}) copy-start(f32[768]{0:T(1024)S(1)} %convert_element_type.174) | copy-start | bytes 9220
  64.8 33.8 %copy-start.62 = (f32[768]{0:T(1024)}, f32[768]{0:T(1024)S(1)}, u32[]{:S(2)}) copy-start(f32[768]{0:T(1024)S(1)} %convert_element_type.175) | copy-start | bytes 9220
  92.6 3.2 copy-start.22
  94.4 4.2 copy-start.8
  94.7 10.3 copy-start.39
  95.8 9.2 copy-start.45
  98.6 19.3 %copy-start.25 = (f32[1024,32]{0,1:T(8,128)}, f32[1024,32]{0,1:T(8,128)S(1)}, u32[]{:S(2)}) copy-start(f32[1024,32]{0,1:T(8,128)S(1)} %get-tuple-element.428) | copy-start | bytes 393220
  123.7 23.4 %copy-start.7 = (bf16[1024,12,64]{0,2,1:T(8,128)(2,1)S(1)}, bf16[1024,12,64]{0,2,1:T(8,128)(2,1)}, u32[]{:S(2)}) copy-start(bf16[1024,12,64]{0,2,1:T(8,128)(2,1)} %get-tuple-element.636) | copy-start | bytes 4718596 | tf_op jit(solution)/shard_map/while
  134.7 15.6 %copy-start = (f32[12,512,1024]{2,1,0:T(8,128)S(1)}, f32[12,512,1024]{2,1,0:T(8,128)}, u32[]{:S(2)}) copy-start(f32[12,512,1024]{2,1,0:T(8,128)} %get-tuple-element.584) | copy-start | bytes 75497472 | tf_op jit(solution)/shard_map/while
  160.8 23.0 %copy-start.7 = (bf16[1024,12,64]{0,2,1:T(8,128)(2,1)S(1)}, bf16[1024,12,64]{0,2,1:T(8,128)(2,1)}, u32[]{:S(2)}) copy-start(bf16[1024,12,64]{0,2,1:T(8,128)(2,1)} %get-tuple-element.636) | copy-start | bytes 4718596 | tf_op jit(solution)/shard_map/while
  171.5 15.6 %copy-start = (f32[12,512,1024]{2,1,0:T(8,128)S(1)}, f32[12,512,1024]{2,1,0:T(8,128)}, u32[]{:S(2)}) copy-start(f32[12,512,1024]{2,1,0:T(8,128)} %get-tuple-element.584) | copy-start | bytes 75497472 | tf_op jit(solution)/shard_map/while
  195.6 5.8 copy-start.1
  195.6 5.8 copy-start.5
  195.6 5.8 copy-start.33
  195.6 5.8 copy-start.35
  195.7 5.8 copy-start.37
  195.7 5.8 copy-start.66
  195.7 5.8 copy-start.64
  205.3 113.1 %copy-start.12 = (f32[1024,768]{0,1:T(8,128)}, f32[1024,768]{0,1:T(8,128)S(1)}, u32[]{:S(2)}) copy-start(f32[1024,768]{0,1:T(8,128)S(1)} %get-tuple-element.432) | copy-start | bytes 9437188
  205.3 113.0 %copy-start.43 = (f32[1024]{0:T(1024)}, f32[1024]{0:T(1024)S(1)}, u32[]{:S(2)}) copy-start(f32[1024]{0:T(1024)S(1)} %broadcast_multiply_fusion) | copy-start | bytes 12292
  205.8 112.6 %copy-start.53 = (f32[1024]{0:T(1024)}, f32[1024]{0:T(1024)S(1)}, u32[]{:S(2)}) copy-start(f32[1024]{0:T(1024)S(1)} %fusion.62) | copy-start | bytes 12292
  314.8 3.6 copy-start.14
  319.3 1.7 copy-start.11
  319.3 1.7 copy-start.47
  319.8 2.0 copy-start.24
  329.3 1.6 copy-start.2
  329.3 1.6 copy-start.28
  330.9 378.7 %reduce-scatter.5.cloned.1.call-start = ((), (), s32[]{:S(2)}) async-start(), calls=%async_computation.8 | async-start | bytes 7962624 | tf_op jit(solution)/shard_map/reduce_scatter | solution.py:320
  333.2 11.4 %copy-start.15 = (bf16[2,512,12,64]{1,3,2,0:T(8,128)(2,1)S(1)}, bf16[2,512,12,64]{1,3,2,0:T(8,128)(2,1)}, u32[]{:S(2)}) copy-start(bf16[2,512,12,64]{1,3,2,0:T(8,128)(2,1)} %get-tuple-element.682) | copy-start | bytes 4718596 | tf_op jit(solution)/shard_map/while
  398.4 9.8 copy-start.6
  408.2 8.7 copy-start.4
  449.4 11.4 %copy-start.15 = (bf16[2,512,12,64]{1,3,2,0:T(8,128)(2,1)S(1)}, bf16[2,512,12,64]{1,3,2,0:T(8,128)(2,1)}, u32[]{:S(2)}) copy-start(bf16[2,512,12,64]{1,3,2,0:T(8,128)(2,1)} %get-tuple-element.682) | copy-start | bytes 4718596 | tf_op jit(solution)/shard_map/while
  514.4 9.8 copy-start.6
  524.2 9.6 copy-start.4
  568.9 2.8 copy-start.3
  568.9 2.8 copy-start.26
  568.9 2.8 copy-start.30
  571.2 1.9 copy-start.18
  572.8 2.0 copy-start.9
  572.8 2.0 copy-start.40
  572.8 2.0 copy-start.42
  572.8 2.0 copy-start.46
  572.8 2.0 copy-start.63
  573.1 1.6 copy-start.21
  581.8 294.4 %reduce-scatter.9.cloned.1.call-start = ((), (), s32[]{:S(2)}) async-start(), calls=%async_computation.10 | async-start | bytes 10616832 | tf_op jit(solution)/shard_map/reduce_scatter | solution.py:285
  593.0 449.8 %reduce-scatter.11.cloned.1.call-start = ((), (), s32[]{:S(2)}) async-start(), calls=%async_computation.11 | async-start | bytes 10616832 | tf_op jit(solution)/shard_map/reduce_scatter | solution.py:287
  604.6 2.3 copy-start.65
  604.6 2.4 copy-start.19
  604.7 500.2 %all-reduce.21.cloned.1.call-start = ((), (), s32[]{:S(2)}) async-start(), calls=%async_computation.12 | async-start | bytes 3538944 | tf_op jit(solution)/shard_map/psum | solution.py:328
  619.3 2.7 copy-start.50
  619.3 3.1 copy-start.10
  622.0 2.0 copy-start.13
  1045.0 5.4 copy-start.17
  1045.0 5.4 copy-start.48
  1050.4 5.9 copy-start.55
  1050.4 5.9 copy-start.56
  1050.4 5.9 copy-start.58
  1050.5 5.9 copy-start.59
  1104.9 5.9 copy-start.29
  (18 other events, 19.0 us)
Sparse Core Ops, SparseCore 0:
  10.2 68.4 all-gather.5
  80.9 39.8 all-gather.7
  123.0 78.6 all-gather.9
  203.8 78.0 all-gather.11
  331.0 67.1 reduce-scatter.6
  582.0 127.5 reduce-scatter.4
  713.6 162.5 reduce-scatter.8
  880.2 162.5 reduce-scatter.10
  1046.8 45.7 all-reduce.20
where the time goes:
time: 1130 us; the launch traced here: 1120 us
  waiting for transfers between devices  444 us (39%)
  matrix products  293 us (26%)
  local copies, waits for them, and re-layouts  129 us (11%)
  other arithmetic  127 us (11%)
  blocking collectives  107 us (9%)
  between operations  18.4 us (2%)
    reduce_scatter x1, waiting for transfers between devices, body(): lax.psum_scatter(grad_up_weight, 'fsdp', scatter_dimension=0, tiled=True)  165 us
    reduce_scatter x1, waiting for transfers between devices, body(): lax.psum_scatter(grad_down_weight, 'fsdp', scatter_dimension=0, tiled=True)  164 us
    unnamed x2, blocking collectives  75.2 us
    reduce_scatter x1, waiting for transfers between devices, body(): lax.psum_scatter(grad_qkv_weight, 'fsdp', scatter_dimension=0, tiled=True)  74.5 us
    dynamic_update_slice x4, local copies, waits for them, and re-layouts, attend_forward(): lax.scan(one_block, jnp.zeros((), jnp.float32), split_blocks(queries, seg...  60.9 us
    dot_general x4, matrix products, block_scores(): jnp.einsum('qhd,khd->hqk', block_queries, key_rows, preferred_element_typ...  44.4 us
    convert_element_type x2, other arithmetic, one_block(): score_grad = (weights * (weight_grad - row_dot)).astype(jnp.bfloat16)  43 us
    dot_general x4, matrix products, times_transpose(): lax.dot_general(left_matrix, right_matrix, (((1,), (1,)), ((), ())), pref...  40.8 us
  transfers between devices with their start and end apart: 9, of which 4 were waited for; matrix products, arithmetic and copies ran while one was open for 43% of the time, Pallas kernels for 0%

commit v1 on v0

--- a/solution.py
+++ b/solution.py
@@ -3,6 +3,7 @@
 import jax.numpy as jnp
 from jax import lax
 from jax.sharding import PartitionSpec as P
+from jax.lax import axis_index, axis_size, ppermute
 
 HEADS = 12
 HEAD_DIM = 64
@@ -211,12 +212,37 @@
         lax.all_gather(w_out, "fsdp", axis=0, tiled=True),
         lax.all_gather(b_out, "fsdp", axis=0, tiled=True),
     )
+
+    def detail_scenes_in(inner_x, axis_key):
+        small = axis_index(axis_key)
+        local_next = axis_size(axis_key)
+        outcome_arr, res, all_values = (local_next, small, inner_x.shape[0])
+        steps_seen = [(to_i, (to_i + 1) % outcome_arr) for to_i in range(outcome_arr)]
+        cards = [(to_i, (to_i - 1) % outcome_arr) for to_i in range(outcome_arr)]
+        reply = jnp.zeros(
+            (*inner_x.shape[:0], outcome_arr * all_values, *inner_x.shape[1:]), inner_x.dtype
+        )
+        reply = lax.dynamic_update_slice_in_dim(reply, inner_x, res * all_values, axis=0)
+        m_next = outcome_arr // 2
+        clean = u1 = inner_x
+        for dd in [*range(1, m_next + 1)]:
+            clean = ppermute(clean, axis_key, steps_seen)
+            reply = lax.dynamic_update_slice_in_dim(
+                reply, clean, (res - dd) % outcome_arr * all_values, axis=0
+            )
+            if dd < outcome_arr - m_next:
+                u1 = ppermute(u1, axis_key, cards)
+                reply = lax.dynamic_update_slice_in_dim(
+                    reply, u1, (res + dd) % outcome_arr * all_values, axis=0
+                )
+        return reply
+
     gain_two, bias_two, up_weight, up_bias, down_weight, down_bias = (
         lax.all_gather(ln2_gain, "fsdp", axis=0, tiled=True),
         lax.all_gather(ln2_bias, "fsdp", axis=0, tiled=True),
         lax.all_gather(w_up, "fsdp", axis=0, tiled=True),
         lax.all_gather(b_up, "fsdp", axis=0, tiled=True),
-        lax.all_gather(w_down, "fsdp", axis=0, tiled=True),
+        detail_scenes_in(w_down, "fsdp"),
         lax.all_gather(b_down, "fsdp", axis=0, tiled=True),
     )
     length = layer_input.shape[1]

time: 1130 us -> 1200 us (1.062)
  starting transfers between devices: 0.53 us -> 34 us
  waiting for transfers between devices: 444 us -> 466 us
  local copies, waits for them, and re-layouts: 129 us -> 145 us
    ppermute x0 -> x7, waiting for transfers between devices: none -> 73.5 us  [the longest x4 72 us: detail_scenes_in(): clean = ppermute(clean, axis_key, steps_seen)]
    reduce_scatter x1, waiting for transfers between devices: 74.5 us -> 21.7 us  [body(): lax.psum_scatter(grad_qkv_weight, 'fsdp', scatter_dimension=0, tiled=True)]
    ppermute x0 -> x7, starting transfers between devices: none -> 33.6 us  [the longest x3 30.4 us: detail_scenes_in(): u1 = ppermute(u1, axis_key, cards)]
    unnamed x158 -> x176, local copies, waits for them, and re-layouts: 28.4 us -> 27 us
  transfers between devices with their start and end apart: 9 -> 16, of which waited for: 4 -> 9; matrix products, arithmetic and copies ran while one was open for 43% -> 42% of each run, Pallas kernels for 0% -> 0%
where the time goes in v1:
time: 1200 us; the launch traced here: 1190 us
  waiting for transfers between devices  466 us (39%)
  matrix products  290 us (24%)
  local copies, waits for them, and re-layouts  145 us (12%)
  other arithmetic  125 us (10%)
  blocking collectives  107 us (9%)
  starting transfers between devices  34 us (3%)
  between operations  18.3 us (2%)
    reduce_scatter x1, waiting for transfers between devices, body(): lax.psum_scatter(grad_up_weight, 'fsdp', scatter_dimension=0, tiled=True)  165 us
    reduce_scatter x1, waiting for transfers between devices, body(): lax.psum_scatter(grad_down_weight, 'fsdp', scatter_dimension=0, tiled=True)  164 us
    unnamed x2, blocking collectives  75.3 us
    ppermute x4, waiting for transfers between devices, detail_scenes_in(): clean = ppermute(clean, axis_key, steps_seen)  72 us
    dynamic_update_slice x4, local copies, waits for them, and re-layouts, attend_forward(): lax.scan(one_block, jnp.zeros((), jnp.float32), split_blocks(queries, seg...  63.7 us
    dot_general x4, matrix products, block_scores(): jnp.einsum('qhd,khd->hqk', block_queries, key_rows, preferred_element_typ...  45.1 us
    convert_element_type x2, other arithmetic, one_block(): score_grad = (weights * (weight_grad - row_dot)).astype(jnp.bfloat16)  43.3 us
    all_gather x1, waiting for transfers between devices, body(): lax.all_gather(w_down, 'fsdp', axis=0, tiled=True)  38.8 us
  transfers between devices with their start and end apart: 16, of which 9 were waited for; matrix products, arithmetic and copies ran while one was open for 42% of the time, Pallas kernels for 0%

profile of v1, /device:TPU:0, one launch (start us, length us, event | category | flops | bytes accessed | tf_op | source)
XLA Modules:
  0.0 1186.8 jit_solution(7318314022663115308)
XLA Ops:
  18.7 39.6 %all-reduce.16 = (bf16[768]{0:T(1024)(128)(2,1)}, bf16[2304]{0:T(1024)(128)(2,1)S(1)}, bf16[768]{0:T(1024)(128)(2,1)S(1)}, bf16[768]{0:T(1024)(128)(2,1)S(1)}, b...) all-reduce(bf16[768]{0:T(1024)(128)(2,1)S(1)} %dynamic-update-slice, ...), channel_id=1, replica_groups=mesh['fsdp'=8,'replica'=4] {'fsdp'}, use_global_device_ids=true, to_apply=%add.6 | all-reduce | flops 6912 | bytes 27648
  65.0 26.1 %all-gather = bf16[8,1,384]{2,1,0:T(2,128)(2,1)S(1)} all-gather(bf16[1,1,384]{2,1,0:T(2,128)(2,1)S(1)} %reshape.495), channel_id=1, replica_groups=mesh['fsdp'=8,'replica'=4] {'fsdp'}, dimensions={0}, use_global_device_ids=true | all-gather | bytes 6912 | tf_op jit(solution)/shard_map/all_gather | solution.py:244
  94.6 6.3 convolution_add_fusion
  100.9 3.1 fusion.72
  107.7 3.6 copy.88
  111.3 4.3 subtract_convert_fusion.2
  120.1 74.2 %while.27 = (s32[]{:T(128)}, bf16[2,512,12,64]{1,3,2,0:T(8,128)(2,1)}, f32[2,12,512]{2,1,0:T(8,128)S(1)}, s32[2,512]{1,0:T(2,128)S(1)}, s32[1,1024]{1,0:T(1,128)...) while((s32[]{:T(128)}, ...), condition=%wide.region_8.9_spmd, body=%wide.region_5.8_spmd.sunk | while | flops 1688727552 | bytes 190299856 | solution.py:121
  122.4 11.0 fusion.120
  133.4 12.4 %fusion.121 = f32[12,512]{1,0:T(8,128)S(1)} fusion(f32[12,512,1024]{2,1,0:T(8,128)} %get-tuple-element.584, f32[12,512]{1,0:T(8,128)S(1)} %get-tuple-element.585, pred[512,1024]{1,0:T(8,128)(4,1)S(1)} %fusion.119), kind=kLoop, calls=%fused_computation.4.clone.1 | loop fusion | flops 25159680 | bytes 25739264 | tf_op jit(solution)/shard_map/while/body/eval_jaxpr/reduce_sum | solution.py:113
  145.9 3.2 copy-done
  149.0 8.5 bitcast_dynamic-update-slice_fusion.6
  159.6 10.7 fusion.120
  170.3 12.4 %fusion.121 = f32[12,512]{1,0:T(8,128)S(1)} fusion(f32[12,512,1024]{2,1,0:T(8,128)} %get-tuple-element.584, f32[12,512]{1,0:T(8,128)S(1)} %get-tuple-element.585, pred[512,1024]{1,0:T(8,128)(4,1)S(1)} %fusion.119), kind=kLoop, calls=%fused_computation.4.clone.1 | loop fusion | flops 25159680 | bytes 25739264 | tf_op jit(solution)/shard_map/while/body/eval_jaxpr/reduce_sum | solution.py:113
  182.7 3.1 copy-done
  185.8 8.5 bitcast_dynamic-update-slice_fusion.6
  194.3 4.2 copy.90
  200.1 3.8 fusion.74
  204.8 38.1 %multiply_convert_fusion.1 = (bf16[1024,3072]{1,0:T(8,128)(2,1)}, f32[1024,3072]{1,0:T(8,128)}, f32[1024,3072]{1,0:T(8,128)}) fusion(f32[3072]{0:T(1024)S(1)} %bitcast.217, bf16[768,3072]{1,0:T(8,128)(2,1)} %all-gather.10.cloned.1.call-done, f32[1024,768]{0,1:T(8,128)S(1)} %get-tuple-element.432, f32[768]{0:T(1024)S(1)} %copy-done.69, ...), kind=kOutput, calls=%fused_computation.56 | convolution fusion | flops 5043388416 | bytes 39348224 | tf_op jit(solution)/shard_map/dot_general | solution.py:283
  242.8 38.8 %all-gather.12.cloned.1.call-done = bf16[3072,768]{1,0:T(8,128)(2,1)} async-done(((bf16[384,768]{1,0:T(8,128)(2,1)}), bf16[3072,768]{1,0:T(8,128)(2,1)}) %all-gather.12.cloned.1.call-update) | async-done | bytes 4718608 | tf_op jit(solution)/shard_map/all_gather | solution.py:295
  281.6 18.9 %convert_reduce_fusion = (f32[3072]{0:T(1024)}, bf16[1024,3072]{1,0:T(8,128)(2,1)}) fusion(f32[1024,3072]{1,0:T(8,128)} %get-tuple-element.405, bf16[3072,768]{1,0:T(8,128)(2,1)} %all-gather.12.cloned.1.call-done, bf16[1,1024,768]{2,1,0:T(8,128)(2,1)} %param.21, f32[1024,3072]{1,0:T(8,128)} %get-tuple-element.433, f32[3072]{0:T(1024)S(1)} %bitcast.218), kind=kOutput, calls=%fused_computation.54 | convolution fusion | flops 4885312512 | bytes 37773312 | tf_op jit(solution)/shard_map/dot_general | solution.py:22
  300.5 10.3 fusion.76
  310.9 3.5 copy.93
  314.4 3.5 multiply_reduce_fusion.1
  321.4 3.0 fusion.77
  324.4 2.7 convolution_convert_fusion
  330.4 2.9 copy.95
  333.3 237.1 %while.28 = (s32[]{:T(128)}, f32[1024,12,64]{0,2,1:T(8,128)}, f32[1024,12,64]{0,2,1:T(8,128)}, f32[2,512,12,64]{1,0,3,2:T(2,128)}, bf16[2,512,12,64]{1,3,2,0:T(8...) while((s32[]{:T(128)}, f32[1024,12,64]{0,2,1:T(8,128)}, ...), condition=%wide.region_15.16_spmd.clone, body=%wide.region_13.15_spmd.clone.sunk | while | flops 4127846400 | bytes 229843728 | solution.py:185
  335.8 11.8 fusion.131
  347.6 18.2 %multiply_reduce_fusion.5 = (f32[12,512]{1,0:T(8,128)S(1)}, f32[12,512,1024]{2,1,0:T(8,128)}) fusion(f32[12,512,1024]{2,1,0:T(8,128)} %fusion.131, f32[12,512]{1,0:T(8,128)S(1)} %dynamic-slice_bitcast_fusion.2, pred[512,1024]{1,0:T(8,128)(4,1)S(1)} %fusion.132, bf16[1024,12,64]{0,2,1:T(8,128)(2,1)} %get-tuple-element.683, ...), kind=kOutput, calls=%fused_computation.21.clone.1 | convolution fusion | flops 836757504 | bytes 53264896 | tf_op jit(solution)/shard_map/while/body/eval_jaxpr/qhd,khd->hqk/dot_general | solution.py:152
  365.8 22.1 %multiply_convert_fusion.3 = bf16[12,512,1024]{2,1,0:T(8,128)(2,1)} fusion(f32[12,512,1024]{2,1,0:T(8,128)} %get-tuple-element.600, f32[12,512,1024]{2,1,0:T(8,128)} %fusion.131, f32[12,512]{1,0:T(8,128)S(1)} %get-tuple-element.601, f32[12,512]{1,0:T(8,128)S(1)} %dynamic-slice_bitcast_fusion.2, pred[512,1024]{1,0:T(8,128)(4,1)S(1)} %fusion.132), kind=kLoop, calls=%fused_computation.20.clone.1 | loop fusion | flops 37748736 | bytes 63488000 | tf_op jit(solution)/shard_map/while/body/eval_jaxpr/convert_element_type | solution.py:156
  387.9 9.7 multiply_bitcast_fusion.2
  397.7 3.0 copy.127
  400.7 28.8 %dynamic_update_slice.59 = f32[2,512,12,64]{1,0,3,2:T(2,128)} dynamic-update-slice(f32[2,512,12,64]{1,0,3,2:T(2,128)} %get-tuple-element.657, f32[1,512,12,64]{1,0,3,2:T(1,128)S(1)} %copy.127, s32[]{:T(128)} %get-tuple-element.654, s32[]{:T(128)} %constant.86.clone.1..sunk, s32[]{:T(128)} %constant.86.clone.1..sunk, s32[]{:T(128)} %constant.86.clone.1..sunk) | dynamic-update-slice | bytes 3145732 | tf_op jit(solution)/shard_map/while/body/jit(dynamic_update_index_in_dim)/dynamic_update_slice | solution.py:121
  429.5 9.0 bitcast_add_fusion.4
  438.5 13.4 %bitcast_add_fusion.5 = f32[1024,12,64]{0,2,1:T(8,128)} fusion(f32[1024,12,64]{0,2,1:T(8,128)} %get-tuple-element.656, f32[12,512,1024]{2,1,0:T(8,128)} %fusion.131, f32[12,512]{1,0:T(8,128)S(1)} %dynamic-slice_bitcast_fusion.2, pred[512,1024]{1,0:T(8,128)(4,1)S(1)} %copy-done.5, pred[]{:T(512)S(6)} %compare.10, ...), kind=kOutput, calls=%fused_computation.26.clone.1 | convolution fusion | flops 832045056 | bytes 32800772 | tf_op jit(solution)/shard_map/while/body/eval_jaxpr/hqk,qhd->khd/dot_general | solution.py:168
  453.9 11.5 fusion.131
  465.4 18.1 %multiply_reduce_fusion.5 = (f32[12,512]{1,0:T(8,128)S(1)}, f32[12,512,1024]{2,1,0:T(8,128)}) fusion(f32[12,512,1024]{2,1,0:T(8,128)} %fusion.131, f32[12,512]{1,0:T(8,128)S(1)} %dynamic-slice_bitcast_fusion.2, pred[512,1024]{1,0:T(8,128)(4,1)S(1)} %fusion.132, bf16[1024,12,64]{0,2,1:T(8,128)(2,1)} %get-tuple-element.683, ...), kind=kOutput, calls=%fused_computation.21.clone.1 | convolution fusion | flops 836757504 | bytes 53264896 | tf_op jit(solution)/shard_map/while/body/eval_jaxpr/qhd,khd->hqk/dot_general | solution.py:152
  483.5 21.2 %multiply_convert_fusion.3 = bf16[12,512,1024]{2,1,0:T(8,128)(2,1)} fusion(f32[12,512,1024]{2,1,0:T(8,128)} %get-tuple-element.600, f32[12,512,1024]{2,1,0:T(8,128)} %fusion.131, f32[12,512]{1,0:T(8,128)S(1)} %get-tuple-element.601, f32[12,512]{1,0:T(8,128)S(1)} %dynamic-slice_bitcast_fusion.2, pred[512,1024]{1,0:T(8,128)(4,1)S(1)} %fusion.132), kind=kLoop, calls=%fused_computation.20.clone.1 | loop fusion | flops 37748736 | bytes 63488000 | tf_op jit(solution)/shard_map/while/body/eval_jaxpr/convert_element_type | solution.py:156
  504.7 9.6 multiply_bitcast_fusion.2
  514.3 3.0 copy.127
  517.4 28.8 %dynamic_update_slice.59 = f32[2,512,12,64]{1,0,3,2:T(2,128)} dynamic-update-slice(f32[2,512,12,64]{1,0,3,2:T(2,128)} %get-tuple-element.657, f32[1,512,12,64]{1,0,3,2:T(1,128)S(1)} %copy.127, s32[]{:T(128)} %get-tuple-element.654, s32[]{:T(128)} %constant.86.clone.1..sunk, s32[]{:T(128)} %constant.86.clone.1..sunk, s32[]{:T(128)} %constant.86.clone.1..sunk) | dynamic-update-slice | bytes 3145732 | tf_op jit(solution)/shard_map/while/body/jit(dynamic_update_index_in_dim)/dynamic_update_slice | solution.py:121
  546.2 9.9 bitcast_add_fusion.4
  556.0 14.3 %bitcast_add_fusion.5 = f32[1024,12,64]{0,2,1:T(8,128)} fusion(f32[1024,12,64]{0,2,1:T(8,128)} %get-tuple-element.656, f32[12,512,1024]{2,1,0:T(8,128)} %fusion.131, f32[12,512]{1,0:T(8,128)S(1)} %dynamic-slice_bitcast_fusion.2, pred[512,1024]{1,0:T(8,128)(4,1)S(1)} %copy-done.5, pred[]{:T(512)S(6)} %compare.10, ...), kind=kOutput, calls=%fused_computation.26.clone.1 | convolution fusion | flops 832045056 | bytes 32800772 | tf_op jit(solution)/shard_map/while/body/eval_jaxpr/hqk,qhd->khd/dot_general | solution.py:168
  570.5 4.3 reshape.470
  580.2 7.0 fusion.63
  588.0 10.6 fusion.67
  598.6 9.9 fusion.55
  609.2 4.2 collective-permute-start.1
  613.4 26.4 %collective-permute-done = bf16[384,768]{1,0:T(8,128)(2,1)S(1)} collective-permute-done((bf16[384,768]{1,0:T(8,128)(2,1)}, bf16[384,768]{1,0:T(8,128)(2,1)S(1)}, u32[]{:S(2)}, u32[]{:S(2)}) %collective-permute-start) | collective-permute-done | bytes 589856 | tf_op jit(solution)/shard_map/ppermute | solution.py:229
  642.1 3.2 collective-permute-start.3
  645.3 25.7 %collective-permute-done.2 = bf16[384,768]{1,0:T(8,128)(2,1)} collective-permute-done((bf16[384,768]{1,0:T(8,128)(2,1)S(1)}, bf16[384,768]{1,0:T(8,128)(2,1)}, u32[]{:S(2)}, u32[]{:S(2)}) %collective-permute-start.2) | collective-permute-done | bytes 589856 | tf_op jit(solution)/shard_map/ppermute | solution.py:229
  676.5 23.0 %collective-permute-start.5 = (bf16[384,768]{1,0:T(8,128)(2,1)}, bf16[384,768]{1,0:T(8,128)(2,1)S(1)}, u32[]{:S(2)}, u32[]{:S(2)}) collective-permute-start(bf16[384,768]{1,0:T(8,128)(2,1)} %collective-permute-done.3), channel_id=1, source_target_pairs={{0,28},{4,0},{8,4},{12,8},{16,12},{20,16},{24,20},{28,24},{1,29},{... | collective-permute-start | bytes 1769480 | tf_op jit(solution)/shard_map/ppermute | solution.py:234
  700.3 11.5 collective-permute-done.4
  723.4 8.4 collective-permute-done.6
  732.7 5.6 fusion.75
  738.2 3.6 copy.97
  746.4 9.9 fusion.58
  758.0 21.7 %reduce-scatter.5.cloned.1.call-done = f32[96,2304]{1,0:T(8,128)} async-done(((f32[768,2304]{1,0:T(8,128)}), f32[96,2304]{1,0:T(8,128)}) %reduce-scatter.5.cloned.1.call-update) | async-done | bytes 884752 | tf_op jit(solution)/shard_map/reduce_scatter | solution.py:346
  781.6 164.6 %reduce-scatter.9.cloned.1.call-done = f32[96,3072]{1,0:T(8,128)} async-done(((f32[768,3072]{1,0:T(8,128)}), f32[96,3072]{1,0:T(8,128)}) %reduce-scatter.9.cloned.1.call-update) | async-done | bytes 1179664 | tf_op jit(solution)/shard_map/reduce_scatter | solution.py:311
  948.4 164.4 %reduce-scatter.11.cloned.1.call-done = f32[384,768]{1,0:T(8,128)} async-done(((f32[3072,768]{1,0:T(8,128)}), f32[384,768]{1,0:T(8,128)}) %reduce-scatter.11.cloned.1.call-update) | async-done | bytes 1179664 | tf_op jit(solution)/shard_map/reduce_scatter | solution.py:313
  1115.0 2.9 convert_reduce_fusion.1
  1118.7 4.7 convert_reduce_fusion.2
  1123.5 35.8 %all-reduce.15 = (bf16[768]{0:T(1024)(128)(2,1)S(1)}, bf16[768]{0:T(1024)(128)(2,1)S(1)}, bf16[2304]{0:T(1024)(128)(2,1)S(1)}, bf16[768]{0:T(1024)(128)(2,1)S(1)...) all-reduce(f32[768]{0:T(1024)S(1)} %get-tuple-element.321, ...), channel_id=2, replica_groups=mesh['fsdp'=8,'replica'=4] {'fsdp'}, use_global_device_ids=true, to_apply=%region_19.20.clone | all-reduce | flops 9984 | bytes 59904
  1159.8 5.7 all-reduce.17
  (326 shorter events, 99.5 us)
Async XLA Ops:
  7.2 87.4 %all-gather.6.cloned.1.call-start = ((), (), s32[]{:S(2)}) async-start(), calls=%async_computation.4 | async-start | bytes 3981312 | tf_op jit(solution)/shard_map/all_gather | solution.py:210
  7.9 192.2 %all-gather.8.cloned.1.call-start = ((), (), s32[]{:S(2)}) async-start(), calls=%async_computation.5 | async-start | bytes 1327104 | tf_op jit(solution)/shard_map/all_gather | solution.py:212
  8.7 195.8 %all-gather.10.cloned.1.call-start = ((), (), s32[]{:S(2)}) async-start(), calls=%async_computation.6 | async-start | bytes 5308416 | tf_op jit(solution)/shard_map/all_gather | solution.py:243
  9.4 272.2 %all-gather.12.cloned.1.call-start = ((), (), s32[]{:S(2)}) async-start(), calls=%async_computation.7 | async-start | bytes 5308416 | tf_op jit(solution)/shard_map/all_gather | solution.py:295
  10.0 746.4 %reduce-scatter.7.cloned.1.call-start = ((), (), s32[]{:S(2)}) async-start(), calls=%async_computation.9 | async-start | bytes 2654208 | tf_op jit(solution)/shard_map/reduce_scatter | solution.py:348
  58.2 36.3 %copy-start.48 = (f32[768]{0:T(1024)}, f32[768]{0:T(1024)S(1)}, u32[]{:S(2)}) copy-start(f32[768]{0:T(1024)S(1)} %convert_element_type.174) | copy-start | bytes 9220
  58.2 36.3 %copy-start.67 = (f32[768]{0:T(1024)}, f32[768]{0:T(1024)S(1)}, u32[]{:S(2)}) copy-start(f32[768]{0:T(1024)S(1)} %convert_element_type.175) | copy-start | bytes 9220
  58.3 6.7 copy-start.73
  58.3 33.4 %copy-start.26 = (bf16[1,1024,768]{2,1,0:T(8,128)(2,1)S(1)}, bf16[1,1024,768]{2,1,0:T(8,128)(2,1)}, u32[]{:S(2)}) copy-start(bf16[1,1024,768]{2,1,0:T(8,128)(2,1)} %param.21) | copy-start | bytes 4718596
  60.1 34.4 %copy-start.8 = (bf16[1,1024,768]{1,2,0:T(8,128)(2,1)}, bf16[1,1024,768]{1,2,0:T(8,128)(2,1)S(1)}, u32[]{:S(2)}) copy-start(bf16[1,1024,768]{1,2,0:T(8,128)(2,1)S(1)} %copy.84) | copy-start | bytes 4718596
  60.4 40.5 %copy-start.46 = (f32[1024]{0:T(1024)}, f32[1024]{0:T(1024)S(1)}, u32[]{:S(2)}) copy-start(f32[1024]{0:T(1024)S(1)} %broadcast_multiply_fusion.1) | copy-start | bytes 12292
  60.9 40.0 %copy-start.52 = (f32[1024]{0:T(1024)}, f32[1024]{0:T(1024)S(1)}, u32[]{:S(2)}) copy-start(f32[1024]{0:T(1024)S(1)} %fusion.61) | copy-start | bytes 12292
  94.6 16.8 %copy-start.29 = (f32[1024,32]{0,1:T(8,128)}, f32[1024,32]{0,1:T(8,128)S(1)}, u32[]{:S(2)}) copy-start(f32[1024,32]{0,1:T(8,128)S(1)} %get-tuple-element.428) | copy-start | bytes 393220
  122.4 23.5 %copy-start.7 = (bf16[1024,12,64]{0,2,1:T(8,128)(2,1)S(1)}, bf16[1024,12,64]{0,2,1:T(8,128)(2,1)}, u32[]{:S(2)}) copy-start(bf16[1024,12,64]{0,2,1:T(8,128)(2,1)} %get-tuple-element.636) | copy-start | bytes 4718596 | tf_op jit(solution)/shard_map/while
  133.4 15.6 %copy-start = (f32[12,512,1024]{2,1,0:T(8,128)S(1)}, f32[12,512,1024]{2,1,0:T(8,128)}, u32[]{:S(2)}) copy-start(f32[12,512,1024]{2,1,0:T(8,128)} %get-tuple-element.584) | copy-start | bytes 75497472 | tf_op jit(solution)/shard_map/while
  159.5 23.2 %copy-start.7 = (bf16[1024,12,64]{0,2,1:T(8,128)(2,1)S(1)}, bf16[1024,12,64]{0,2,1:T(8,128)(2,1)}, u32[]{:S(2)}) copy-start(bf16[1024,12,64]{0,2,1:T(8,128)(2,1)} %get-tuple-element.636) | copy-start | bytes 4718596 | tf_op jit(solution)/shard_map/while
  170.3 15.5 %copy-start = (f32[12,512,1024]{2,1,0:T(8,128)S(1)}, f32[12,512,1024]{2,1,0:T(8,128)}, u32[]{:S(2)}) copy-start(f32[12,512,1024]{2,1,0:T(8,128)} %get-tuple-element.584) | copy-start | bytes 75497472 | tf_op jit(solution)/shard_map/while
  194.3 5.8 copy-start.1
  194.3 5.8 copy-start.6
  194.3 5.8 copy-start.39
  194.3 5.8 copy-start.42
  194.3 5.8 copy-start.44
  194.3 5.8 copy-start.75
  194.3 5.8 copy-start.71
  204.0 113.9 %copy-start.13 = (f32[1024,768]{0,1:T(8,128)}, f32[1024,768]{0,1:T(8,128)S(1)}, u32[]{:S(2)}) copy-start(f32[1024,768]{0,1:T(8,128)S(1)} %get-tuple-element.432) | copy-start | bytes 9437188
  204.0 113.9 %copy-start.50 = (f32[1024]{0:T(1024)}, f32[1024]{0:T(1024)S(1)}, u32[]{:S(2)}) copy-start(f32[1024]{0:T(1024)S(1)} %broadcast_multiply_fusion) | copy-start | bytes 12292
  204.4 113.5 %copy-start.60 = (f32[1024]{0:T(1024)}, f32[1024]{0:T(1024)S(1)}, u32[]{:S(2)}) copy-start(f32[1024]{0:T(1024)S(1)} %fusion.62) | copy-start | bytes 12292
  324.4 455.3 %reduce-scatter.5.cloned.1.call-start = ((), (), s32[]{:S(2)}) async-start(), calls=%async_computation.8 | async-start | bytes 7962624 | tf_op jit(solution)/shard_map/reduce_scatter | solution.py:346
  327.9 5.3 copy-start.2
  327.9 5.3 copy-start.32
  327.9 5.3 copy-start.37
  327.9 5.3 copy-start.40
  328.0 5.3 copy-start.43
  328.0 5.3 copy-start.45
  328.0 5.3 copy-start.76
  335.8 30.1 %copy-start.4 = (pred[512,1024]{1,0:T(8,128)(4,1)}, pred[512,1024]{1,0:T(8,128)(4,1)S(1)}, u32[]{:S(2)}) copy-start(pred[512,1024]{1,0:T(8,128)(4,1)S(1)} %fusion.132) | copy-start | bytes 1572868 | tf_op jit(solution)/shard_map/while
  429.5 9.0 copy-start.5
  429.5 9.0 copy-start.16
  453.9 29.6 %copy-start.4 = (pred[512,1024]{1,0:T(8,128)(4,1)}, pred[512,1024]{1,0:T(8,128)(4,1)S(1)}, u32[]{:S(2)}) copy-start(pred[512,1024]{1,0:T(8,128)(4,1)S(1)} %fusion.132) | copy-start | bytes 1572868 | tf_op jit(solution)/shard_map/while
  546.2 9.9 copy-start.5
  546.2 9.9 copy-start.16
  579.0 153.6 %copy-start.21 = (bf16[1024,12,64]{0,2,1:T(8,128)(2,1)}, bf16[1024,12,64]{0,2,1:T(8,128)(2,1)S(1)}, u32[]{:S(2)}) copy-start(bf16[1024,12,64]{0,2,1:T(8,128)(2,1)S(1)} %get-tuple-element.440) | copy-start | bytes 4718596
  587.3 358.9 %reduce-scatter.9.cloned.1.call-start = ((), (), s32[]{:S(2)}) async-start(), calls=%async_computation.10 | async-start | bytes 10616832 | tf_op jit(solution)/shard_map/reduce_scatter | solution.py:311
  598.6 514.2 %reduce-scatter.11.cloned.1.call-start = ((), (), s32[]{:S(2)}) async-start(), calls=%async_computation.11 | async-start | bytes 10616832 | tf_op jit(solution)/shard_map/reduce_scatter | solution.py:313
  608.5 64.4 %copy-start.72 = (bf16[768]{0:T(1024)(128)(2,1)S(1)}, bf16[768]{0:T(1024)(128)(2,1)}, u32[]{:S(2)}) copy-start(bf16[768]{0:T(1024)(128)(2,1)} %get-tuple-element.381) | copy-start | bytes 4612
  608.6 565.4 %all-reduce.21.cloned.1.call-start = ((), (), s32[]{:S(2)}) async-start(), calls=%async_computation.12 | async-start | bytes 3538944 | tf_op jit(solution)/shard_map/psum | solution.py:354
  608.6 31.1 %collective-permute-start = (bf16[384,768]{1,0:T(8,128)(2,1)}, bf16[384,768]{1,0:T(8,128)(2,1)S(1)}, u32[]{:S(2)}, u32[]{:S(2)}) collective-permute-start(bf16[384,768]{1,0:T(8,128)(2,1)} %param.34), channel_id=1, source_target_pairs={{0,4},{4,8},{8,12},{12,16},{16,20},{20,24},{24,28},{28,0},{1,5},{5... | collective-permute-start | bytes 1769480 | tf_op jit(solution)/shard_map/ppermute | solution.py:229
  609.2 32.9 %collective-permute-start.1 = (bf16[384,768]{1,0:T(8,128)(2,1)}, bf16[384,768]{1,0:T(8,128)(2,1)}, u32[]{:S(2)}, u32[]{:S(2)}) collective-permute-start(bf16[384,768]{1,0:T(8,128)(2,1)} %param.34), channel_id=1, source_target_pairs={{0,28},{4,0},{8,4},{12,8},{16,12},{20,16},{24,20},{28,24},{1,29},{... | collective-permute-start | bytes 1769480 | tf_op jit(solution)/shard_map/ppermute | solution.py:234
  640.6 30.5 %collective-permute-start.2 = (bf16[384,768]{1,0:T(8,128)(2,1)S(1)}, bf16[384,768]{1,0:T(8,128)(2,1)}, u32[]{:S(2)}, u32[]{:S(2)}) collective-permute-start(bf16[384,768]{1,0:T(8,128)(2,1)S(1)} %collective-permute-done), channel_id=1, source_target_pairs={{0,4},{4,8},{8,12},{12,16},{16,20},{20,24},{24,28},{28,0},{1,5},{5... | collective-permute-start | bytes 1769480 | tf_op jit(solution)/shard_map/ppermute | solution.py:229
  642.1 34.4 %collective-permute-start.3 = (bf16[384,768]{1,0:T(8,128)(2,1)}, bf16[384,768]{1,0:T(8,128)(2,1)}, u32[]{:S(2)}, u32[]{:S(2)}) collective-permute-start(bf16[384,768]{1,0:T(8,128)(2,1)} %collective-permute-done.1), channel_id=1, source_target_pairs={{0,28},{4,0},{8,4},{12,8},{16,12},{20,16},{24,20},{28,24},{1,29},{... | collective-permute-start | bytes 1769480 | tf_op jit(solution)/shard_map/ppermute | solution.py:234
  671.0 40.7 %collective-permute-start.4 = (bf16[384,768]{1,0:T(8,128)(2,1)}, bf16[384,768]{1,0:T(8,128)(2,1)}, u32[]{:S(2)}, u32[]{:S(2)}) collective-permute-start(bf16[384,768]{1,0:T(8,128)(2,1)} %collective-permute-done.2), channel_id=1, source_target_pairs={{0,4},{4,8},{8,12},{12,16},{16,20},{20,24},{24,28},{28,0},{1,5},{5... | collective-permute-start | bytes 1769480 | tf_op jit(solution)/shard_map/ppermute | solution.py:229
  673.0 26.4 %copy-start.34 = (bf16[384,768]{1,0:T(8,128)(2,1)S(1)}, bf16[384,768]{1,0:T(8,128)(2,1)}, u32[]{:S(2)}) copy-start(bf16[384,768]{1,0:T(8,128)(2,1)} %copy-done.33) | copy-start | bytes 1769476
  676.5 46.0 %collective-permute-start.5 = (bf16[384,768]{1,0:T(8,128)(2,1)}, bf16[384,768]{1,0:T(8,128)(2,1)S(1)}, u32[]{:S(2)}, u32[]{:S(2)}) collective-permute-start(bf16[384,768]{1,0:T(8,128)(2,1)} %collective-permute-done.3), channel_id=1, source_target_pairs={{0,28},{4,0},{8,4},{12,8},{16,12},{20,16},{24,20},{28,24},{1,29},{... | collective-permute-start | bytes 1769480 | tf_op jit(solution)/shard_map/ppermute | solution.py:234
  711.8 20.0 %collective-permute-start.6 = (bf16[384,768]{1,0:T(8,128)(2,1)}, bf16[384,768]{1,0:T(8,128)(2,1)S(1)}, u32[]{:S(2)}, u32[]{:S(2)}) collective-permute-start(bf16[384,768]{1,0:T(8,128)(2,1)} %collective-permute-done.4), channel_id=1, source_target_pairs={{0,4},{4,8},{8,12},{12,16},{16,20},{20,24},{24,28},{28,0},{1,5},{5... | collective-permute-start | bytes 1769480 | tf_op jit(solution)/shard_map/ppermute | solution.py:229
  714.4 18.2 %copy-start.74 = (bf16[768,2304]{1,0:T(8,128)(2,1)S(1)}, bf16[768,2304]{1,0:T(8,128)(2,1)}, u32[]{:S(2)}) copy-start(bf16[768,2304]{1,0:T(8,128)(2,1)} %all-gather.6.cloned.1.call-done) | copy-start | bytes 10616836
  716.5 16.1 %copy-start.20 = (bf16[1024,12,64]{0,2,1:T(8,128)(2,1)S(1)}, bf16[1024,12,64]{0,2,1:T(8,128)(2,1)}, u32[]{:S(2)}) copy-start(bf16[1024,12,64]{0,2,1:T(8,128)(2,1)} %copy-done.19) | copy-start | bytes 4718596
  716.5 16.1 %copy-start.23 = (bf16[1024,12,64]{0,2,1:T(8,128)(2,1)S(1)}, bf16[1024,12,64]{0,2,1:T(8,128)(2,1)}, u32[]{:S(2)}) copy-start(bf16[1024,12,64]{0,2,1:T(8,128)(2,1)} %copy-done.22) | copy-start | bytes 4718596
  1118.7 4.7 copy-start.62
  1118.7 4.7 copy-start.63
  1118.7 4.7 copy-start.65
  1118.7 4.7 copy-start.66
  1123.4 49.0 %copy-start.27 = (bf16[1,1024,768]{1,2,0:T(8,128)(2,1)S(1)}, bf16[1,1024,768]{1,2,0:T(8,128)(2,1)}, u32[]{:S(2)}) copy-start(bf16[1,1024,768]{1,2,0:T(8,128)(2,1)} %fusion.58) | copy-start | bytes 4718596
  1174.0 4.4 copy-start.38
  1174.0 5.4 copy-start.41
  (34 other events, 64.9 us)
Sparse Core Ops, SparseCore 0:
  10.2 68.5 all-gather.5
  81.0 39.6 all-gather.7
  122.8 78.6 all-gather.9
  203.6 78.0 all-gather.11
  324.5 67.1 reduce-scatter.6
  587.4 192.1 reduce-scatter.4
  783.7 162.4 reduce-scatter.8
  950.2 162.5 reduce-scatter.10
  1116.7 45.7 all-reduce.20
